TPU v7x, 768 devices: a whole 4x8x12 slice. The times are simulated.
768 devices in a mesh: dom: 192 (over z, y, core), grid: 4 (over x).
Axes of the slice: x: 4, y: 8, z: 12, core: 2. Of those that a mesh axis runs over, the one named last changes fastest.
Arguments:
- rhs: bfloat16 [4, 1152, 16, 320], P('grid', 'dom'), may hold values from -24 to 24
- blocks: bfloat16 [4, 1152, 3, 320, 320], P('grid', 'dom'), may hold values from -0.1875 to 0.1875
- offsets: int32 [4, 1152, 3], P('grid', 'dom'), may hold values from -1 to 1
- donor_elem: int32 [4, 192, 4, 2], P('grid', 'dom'), may hold values from 0 to 5
- fringe_elem: int32 [4, 192, 4, 2], P('grid', 'dom'), may hold values from 0 to 5
- donor_weight: float32 [4, 192, 4, 2], P('grid', 'dom'), may hold values from 0.25 to 1
- fringe_count: int32 [4, 192, 4], P('grid', 'dom'), may hold values from 0 to 2, as said below
Outputs:
- powers: bfloat16 [4, 1152, 4, 16, 320], P('grid', 'dom')
- r_factor: float32 [80, 80], replicated
Inputs may be any that keep to these rules, and one draw needn't show every extreme that they name: `fringe_count`: the count from a grid to its own partitions is 0. In every draw some partition of each grid receives 2 slots from every other grid.
All inputs are finite; a program needn't handle non-finite values.
Results may differ from a plain program's by a relative error of at most 0.0033.
The roundings to bfloat16 on the way count: a program that leaves them out, or rounds other values in their place, can miss the bound.
Values may be sent and summed in bfloat16 or wider, within the bound.
A program may use at most 32 MiB of HBM per device.

v0:
```python
import jax
import jax.numpy as jnp
from jax import lax
from jax.sharding import PartitionSpec as P

S = 4
H = 1


def extended_2(array, sides, width):
    for axis, dim in sides:
        peers, length = (lax.axis_size(axis), array.shape[dim])
        up = [(i, (i + 1) % peers) for i in range(peers - 1)]
        down = [(j, i) for i, j in up]
        last = lax.slice_in_dim(array, length - width, length, axis=dim)
        leading = lax.slice_in_dim(array, 0, width, axis=dim)
        before = lax.ppermute(last, axis, up)
        after = lax.ppermute(leading, axis, down)
        array = jnp.concatenate([before, array, after], axis=dim)
    return array


def local(rhs, blocks, offsets, donor_elem, fringe_elem, donor_weight, fringe_count):
    elem_count = rhs.shape[1]
    rhs_count = rhs.shape[2]
    unknowns = rhs.shape[3]
    slot_count = donor_elem.shape[3]
    grid_count = lax.axis_size("grid")
    col_index = offsets[0] + jnp.arange(elem_count, dtype=jnp.int32)[:, None] + H
    live_slot = jnp.arange(slot_count, dtype=jnp.int32)[None, :] < fringe_count[0, 0][:, None]
    weights = jnp.where(live_slot, donor_weight[0, 0], 0.0)
    hit_target = (
        fringe_elem[0, 0][None, :, :] == jnp.arange(elem_count, dtype=jnp.int32)[:, None, None]
    )
    spread = jnp.where(hit_target, weights[None], 0.0)
    columns = (S + 1) * rhs_count
    field = rhs[0]
    basis = [field]
    for level in range(S):
        extended = extended_2(field, (("dom", 0),), H)
        taken_cols = extended[col_index]
        blockpart = jnp.einsum(
            "ekra,ekab->erb", taken_cols, blocks[0], preferred_element_type=jnp.float32
        )
        gathered = lax.all_gather(field, "grid", axis=0, tiled=True)
        source_index = (
            jnp.arange(grid_count, dtype=jnp.int32)[:, None] * elem_count + donor_elem[0, 0]
        )
        picked = gathered[source_index]
        donorpart = jnp.einsum(
            "egc,gcrw->erw", spread, picked.astype(jnp.float32), precision=lax.Precision.HIGHEST
        )
        field = (blockpart + donorpart).astype(jnp.bfloat16)
        basis.append(field)
    stacked = jnp.stack(basis, axis=1)
    partial_gram = jnp.einsum(
        "ekrw,elqw->krlq", stacked, stacked, preferred_element_type=jnp.float32
    )
    gram = lax.psum(partial_gram.reshape(columns, columns), ("dom", "grid"))
    row_total = grid_count * lax.axis_size("dom") * elem_count * unknowns
    gram = gram / row_total
    r_factor = jnp.linalg.cholesky(gram).T
    powers = jnp.stack(basis[1:], axis=1)[None]
    return (powers, r_factor)


def solution(mesh):
    in_specs = (
        P("grid", "dom", None, None),
        P("grid", "dom", None, None, None),
        P("grid", "dom", None),
        P("grid", "dom", None, None),
        P("grid", "dom", None, None),
        P("grid", "dom", None, None),
        P("grid", "dom", None),
    )
    out_specs = (P("grid", "dom", None, None, None), P())
    return jax.shard_map(local, mesh=mesh, in_specs=in_specs, out_specs=out_specs, check_vma=False)
```

profile of v0, /device:TPU:1, one launch (start us, length us, event | category | flops | bytes accessed | tf_op | source)
XLA Modules:
  0.0 241.9 jit_solution(4558628184049774057)
XLA Ops:
  0.6 0.7 slice_bitcast_fusion.1
  1.4 4.6 %collective-permute-start = (bf16[1,16,320]{2,1,0:T(8,128)(2,1)S(1)}, bf16[1,16,320]{2,1,0:T(8,128)(2,1)S(1)}, u32[]{:S(2)}, u32[]{:S(2)}) collective-permute-start(bf16[1,16,320]{2,1,0:T(8,128)(2,1)S(1)} %get-tuple-element.14), channel_id=1, source_target_pairs={{0,4},{4,8},{8,12},{12,16},{16,20},{20,24},{24,28},{28,32},{32,36}... | collective-permute-start | bytes 30728 | tf_op jit(solution)/shard_map/ppermute | solution.py:17
  6.0 9.1 %collective-permute-start.1 = (bf16[1,16,320]{2,1,0:T(8,128)(2,1)S(1)}, bf16[1,16,320]{2,1,0:T(8,128)(2,1)S(1)}, u32[]{:S(2)}, u32[]{:S(2)}) collective-permute-start(bf16[1,16,320]{2,1,0:T(8,128)(2,1)S(1)} %get-tuple-element.15), channel_id=1, source_target_pairs={{4,0},{8,4},{12,8},{16,12},{20,16},{24,20},{28,24},{32,28},{36,32}... | collective-permute-start | bytes 30728 | tf_op jit(solution)/shard_map/ppermute | solution.py:18
  15.1 0.9 bitcast_dynamic-update-slice_fusion
  17.7 10.6 %all-gather = bf16[1,24,16,320]{3,2,0,1:T(8,128)(2,1)S(1)} all-gather(bf16[1,6,16,320]{3,2,0,1:T(8,128)(2,1)} %bitcast.166), channel_id=2, replica_groups=mesh['dom'=192,'grid'=4] {'grid'}, dimensions={1}, use_global_device_ids=true | all-gather | bytes 307200 | tf_op jit(solution)/shard_map/all_gather | solution.py:45
  29.6 1.1 convolution_bitcast_fusion.4
  30.7 0.9 pad_maximum_fusion
  32.2 3.0 %constant_dynamic-update-slice_fusion.3 = (bf16[6,5,16,320]{3,2,0,1:T(8,128)(2,1)S(1)}, bf16[6,16,320]{2,1,0:T(8,128)(2,1)S(1)}) fusion(bf16[6,5,16,320]{3,2,0,1:T(8,128)(2,1)S(1)} %bitcast_dynamic-update-slice_fusion, f32[6,16,320]{2,0,1:T(8,128)S(1)} %convolution_bitcast_fusion.4, bf16[6,3,16,320]{3,2,1,0:T(8,128)(2,1)S(1)} %bitcast.165, ...), kind=kOutput, calls=%fused_computation.58 | convolution fusion | flops 59043840 | bytes 4251648 | tf_op jit(solution)/shard_map/ekra,ekab->erb/dot_general | solution.py:42
  35.2 9.4 %all_gather.13 = bf16[24,16,320]{2,1,0:T(8,128)(2,1)S(1)} all-gather(bf16[6,16,320]{2,1,0:T(8,128)(2,1)S(1)} %get-tuple-element.17), channel_id=1, replica_groups=mesh['dom'=192,'grid'=4] {'grid'}, dimensions={0}, use_global_device_ids=true | all-gather | bytes 307200 | tf_op jit(solution)/shard_map/all_gather | solution.py:45
  44.6 1.9 collective-permute-start.2
  46.6 5.8 %collective-permute-start.3 = (bf16[1,16,320]{2,1,0:T(8,128)(2,1)S(1)}, bf16[1,16,320]{2,1,0:T(8,128)(2,1)S(1)}, u32[]{:S(2)}, u32[]{:S(2)}) collective-permute-start(bf16[1,16,320]{2,1,0:T(8,128)(2,1)S(1)} %get-tuple-element.13), channel_id=1, source_target_pairs={{4,0},{8,4},{12,8},{16,12},{20,16},{24,20},{28,24},{32,28},{36,32}... | collective-permute-start | bytes 30728 | tf_op jit(solution)/shard_map/ppermute | solution.py:18
  54.0 3.0 %constant_dynamic-update-slice_fusion.2 = (bf16[6,5,16,320]{3,2,0,1:T(8,128)(2,1)S(1)}, bf16[6,16,320]{2,1,0:T(8,128)(2,1)S(1)}) fusion(bf16[6,5,16,320]{3,2,0,1:T(8,128)(2,1)S(1)} %get-tuple-element.16, f32[6,16,320]{2,0,1:T(8,128)S(1)} %convolution_bitcast_fusion.3, bf16[6,3,16,320]{3,2,1,0:T(8,128)(2,1)S(1)} %bitcast.163, ...), kind=kOutput, calls=%fused_computation.57 | convolution fusion | flops 59043840 | bytes 4251648 | tf_op jit(solution)/shard_map/ekra,ekab->erb/dot_general | solution.py:42
  57.0 9.4 %all_gather.14 = bf16[24,16,320]{2,1,0:T(8,128)(2,1)S(1)} all-gather(bf16[6,16,320]{2,1,0:T(8,128)(2,1)S(1)} %get-tuple-element.19), channel_id=1, replica_groups=mesh['dom'=192,'grid'=4] {'grid'}, dimensions={0}, use_global_device_ids=true | all-gather | bytes 307200 | tf_op jit(solution)/shard_map/all_gather | solution.py:45
  66.4 3.2 %collective-permute-start.4 = (bf16[1,16,320]{2,1,0:T(8,128)(2,1)S(1)}, bf16[1,16,320]{2,1,0:T(8,128)(2,1)S(1)}, u32[]{:S(2)}, u32[]{:S(2)}) collective-permute-start(bf16[1,16,320]{2,1,0:T(8,128)(2,1)S(1)} %get-tuple-element.10), channel_id=1, source_target_pairs={{0,4},{4,8},{8,12},{12,16},{16,20},{20,24},{24,28},{28,32},{32,36}... | collective-permute-start | bytes 30728 | tf_op jit(solution)/shard_map/ppermute | solution.py:17
  69.6 3.3 %collective-permute-start.5 = (bf16[1,16,320]{2,1,0:T(8,128)(2,1)S(1)}, bf16[1,16,320]{2,1,0:T(8,128)(2,1)S(1)}, u32[]{:S(2)}, u32[]{:S(2)}) collective-permute-start(bf16[1,16,320]{2,1,0:T(8,128)(2,1)S(1)} %get-tuple-element.11), channel_id=1, source_target_pairs={{4,0},{8,4},{12,8},{16,12},{20,16},{24,20},{28,24},{32,28},{36,32}... | collective-permute-start | bytes 30728 | tf_op jit(solution)/shard_map/ppermute | solution.py:18
  75.3 3.0 %constant_dynamic-update-slice_fusion.1 = (bf16[6,5,16,320]{3,2,0,1:T(8,128)(2,1)S(1)}, bf16[6,16,320]{2,1,0:T(8,128)(2,1)S(1)}) fusion(bf16[6,5,16,320]{3,2,0,1:T(8,128)(2,1)S(1)} %get-tuple-element.18, f32[6,16,320]{2,0,1:T(8,128)S(1)} %convolution_bitcast_fusion.2, bf16[6,3,16,320]{3,2,1,0:T(8,128)(2,1)S(1)} %bitcast.164, ...), kind=kOutput, calls=%fused_computation.56 | convolution fusion | flops 59043840 | bytes 4251648 | tf_op jit(solution)/shard_map/ekra,ekab->erb/dot_general | solution.py:42
  78.3 10.5 %all_gather.15 = bf16[24,16,320]{2,1,0:T(8,128)(2,1)S(1)} all-gather(bf16[6,16,320]{2,1,0:T(8,128)(2,1)S(1)} %get-tuple-element.21), channel_id=1, replica_groups=mesh['dom'=192,'grid'=4] {'grid'}, dimensions={0}, use_global_device_ids=true | all-gather | bytes 307200 | tf_op jit(solution)/shard_map/all_gather | solution.py:45
  88.8 3.9 %collective-permute-start.6 = (bf16[1,16,320]{2,1,0:T(8,128)(2,1)S(1)}, bf16[1,16,320]{2,1,0:T(8,128)(2,1)S(1)}, u32[]{:S(2)}, u32[]{:S(2)}) collective-permute-start(bf16[1,16,320]{2,1,0:T(8,128)(2,1)S(1)} %get-tuple-element.8), channel_id=1, source_target_pairs={{0,4},{4,8},{8,12},{12,16},{16,20},{20,24},{24,28},{28,32},{32,36}... | collective-permute-start | bytes 30728 | tf_op jit(solution)/shard_map/ppermute | solution.py:17
  92.7 1.9 collective-permute-start.7
  95.6 2.1 collective-permute-done.7
  98.4 3.0 %constant_dynamic-update-slice_fusion = (bf16[6,5,16,320]{3,2,0,1:T(8,128)(2,1)S(1)}, bf16[6,1,16,320]{3,2,0,1:T(8,128)(2,1)S(1)}) fusion(bf16[6,5,16,320]{3,2,0,1:T(8,128)(2,1)S(1)} %get-tuple-element.20, f32[6,16,320]{2,0,1:T(8,128)S(1)} %convolution_bitcast_fusion.1, bf16[6,3,16,320]{3,2,1,0:T(8,128)(2,1)S(1)} %bitcast.162, ...), kind=kOutput, calls=%fused_computation.55 | convolution fusion | flops 59043840 | bytes 4251648 | tf_op jit(solution)/shard_map/ekra,ekab->erb/dot_general | solution.py:42
  102.1 0.7 copy.52
  103.2 129.3 %psum.7 = f32[80,80]{0,1:T(8,128)S(1)} all-reduce(f32[80,80]{0,1:T(8,128)S(1)} %reshape.201), channel_id=1, replica_groups=mesh['dom'=192,'grid'=4] {'dom','grid'}, use_global_device_ids=true, to_apply=%region_0.1 | all-reduce | flops 6400 | bytes 51200 | tf_op jit(solution)/shard_map/psum | solution.py:59
  232.5 7.3 %cholesky.18 = f32[80,80]{1,0:T(8,128)S(1)} custom-call(f32[80,80]{1,0:T(8,128)S(1)} %fusion.53), custom_call_target="Cholesky" | custom-call | tf_op jit(solution)/shard_map/jit(cholesky)/cholesky | solution.py:62
  (47 shorter events, 12.2 us)
Async XLA Ops:
  0.6 52.3 %copy-start = (s32[1,1,4,2]{2,3,1,0:T(2,128)S(1)}, s32[1,1,4,2]{2,3,1,0:T(2,128)}, u32[]{:S(2)}) copy-start(s32[1,1,4,2]{2,3,1,0:T(2,128)} %param.11) | copy-start | bytes 100
  1.4 29.3 %collective-permute-start = (bf16[1,16,320]{2,1,0:T(8,128)(2,1)S(1)}, bf16[1,16,320]{2,1,0:T(8,128)(2,1)S(1)}, u32[]{:S(2)}, u32[]{:S(2)}) collective-permute-start(bf16[1,16,320]{2,1,0:T(8,128)(2,1)S(1)} %get-tuple-element.14), channel_id=1, source_target_pairs={{0,4},{4,8},{8,12},{12,16},{16,20},{20,24},{24,28},{28,32},{32,36}... | collective-permute-start | bytes 30728 | tf_op jit(solution)/shard_map/ppermute | solution.py:17
  6.0 24.7 %collective-permute-start.1 = (bf16[1,16,320]{2,1,0:T(8,128)(2,1)S(1)}, bf16[1,16,320]{2,1,0:T(8,128)(2,1)S(1)}, u32[]{:S(2)}, u32[]{:S(2)}) collective-permute-start(bf16[1,16,320]{2,1,0:T(8,128)(2,1)S(1)} %get-tuple-element.15), channel_id=1, source_target_pairs={{4,0},{8,4},{12,8},{16,12},{20,16},{24,20},{28,24},{32,28},{36,32}... | collective-permute-start | bytes 30728 | tf_op jit(solution)/shard_map/ppermute | solution.py:18
  44.6 8.7 %collective-permute-start.2 = (bf16[1,16,320]{2,1,0:T(8,128)(2,1)S(1)}, bf16[1,16,320]{2,1,0:T(8,128)(2,1)S(1)}, u32[]{:S(2)}, u32[]{:S(2)}) collective-permute-start(bf16[1,16,320]{2,1,0:T(8,128)(2,1)S(1)} %get-tuple-element.12), channel_id=1, source_target_pairs={{0,4},{4,8},{8,12},{12,16},{16,20},{20,24},{24,28},{28,32},{32,36}... | collective-permute-start | bytes 30728 | tf_op jit(solution)/shard_map/ppermute | solution.py:17
  46.6 6.8 %collective-permute-start.3 = (bf16[1,16,320]{2,1,0:T(8,128)(2,1)S(1)}, bf16[1,16,320]{2,1,0:T(8,128)(2,1)S(1)}, u32[]{:S(2)}, u32[]{:S(2)}) collective-permute-start(bf16[1,16,320]{2,1,0:T(8,128)(2,1)S(1)} %get-tuple-element.13), channel_id=1, source_target_pairs={{4,0},{8,4},{12,8},{16,12},{20,16},{24,20},{28,24},{32,28},{36,32}... | collective-permute-start | bytes 30728 | tf_op jit(solution)/shard_map/ppermute | solution.py:18
  66.4 7.4 %collective-permute-start.4 = (bf16[1,16,320]{2,1,0:T(8,128)(2,1)S(1)}, bf16[1,16,320]{2,1,0:T(8,128)(2,1)S(1)}, u32[]{:S(2)}, u32[]{:S(2)}) collective-permute-start(bf16[1,16,320]{2,1,0:T(8,128)(2,1)S(1)} %get-tuple-element.10), channel_id=1, source_target_pairs={{0,4},{4,8},{8,12},{12,16},{16,20},{20,24},{24,28},{28,32},{32,36}... | collective-permute-start | bytes 30728 | tf_op jit(solution)/shard_map/ppermute | solution.py:17
  69.6 5.0 %collective-permute-start.5 = (bf16[1,16,320]{2,1,0:T(8,128)(2,1)S(1)}, bf16[1,16,320]{2,1,0:T(8,128)(2,1)S(1)}, u32[]{:S(2)}, u32[]{:S(2)}) collective-permute-start(bf16[1,16,320]{2,1,0:T(8,128)(2,1)S(1)} %get-tuple-element.11), channel_id=1, source_target_pairs={{4,0},{8,4},{12,8},{16,12},{20,16},{24,20},{28,24},{32,28},{36,32}... | collective-permute-start | bytes 30728 | tf_op jit(solution)/shard_map/ppermute | solution.py:18
  88.8 6.8 %collective-permute-start.6 = (bf16[1,16,320]{2,1,0:T(8,128)(2,1)S(1)}, bf16[1,16,320]{2,1,0:T(8,128)(2,1)S(1)}, u32[]{:S(2)}, u32[]{:S(2)}) collective-permute-start(bf16[1,16,320]{2,1,0:T(8,128)(2,1)S(1)} %get-tuple-element.8), channel_id=1, source_target_pairs={{0,4},{4,8},{8,12},{12,16},{16,20},{20,24},{24,28},{28,32},{32,36}... | collective-permute-start | bytes 30728 | tf_op jit(solution)/shard_map/ppermute | solution.py:17
  92.7 5.0 %collective-permute-start.7 = (bf16[1,16,320]{2,1,0:T(8,128)(2,1)S(1)}, bf16[1,16,320]{2,1,0:T(8,128)(2,1)S(1)}, u32[]{:S(2)}, u32[]{:S(2)}) collective-permute-start(bf16[1,16,320]{2,1,0:T(8,128)(2,1)S(1)} %get-tuple-element.9), channel_id=1, source_target_pairs={{4,0},{8,4},{12,8},{16,12},{20,16},{24,20},{28,24},{32,28},{36,32}... | collective-permute-start | bytes 30728 | tf_op jit(solution)/shard_map/ppermute | solution.py:18
where the time goes:
time: 243 us; the launch traced here: 242 us
  blocking collectives  169 us (70%)
  starting transfers between devices  33.7 us (14%)
  matrix products  14.9 us (6%)
  other arithmetic  11.8 us (5%)
  local copies, waits for them, and re-layouts  8.49 us (3%)
  waiting for transfers between devices  2.86 us (1%)
    psum x1, blocking collectives, local(): gram = lax.psum(partial_gram.reshape(columns, columns), ('dom', 'grid'))  129 us
    all_gather x4, blocking collectives, local(): gathered = lax.all_gather(field, 'grid', axis=0, tiled=True)  40 us
    ppermute x4, starting transfers between devices, extended_2(): after = lax.ppermute(leading, axis, down)  20.1 us
    ppermute x4, starting transfers between devices, extended_2(): before = lax.ppermute(last, axis, up)  13.6 us
    dot_general x4, matrix products, local(): jnp.einsum('ekra,ekab->erb', taken_cols, blocks[0], preferred_element_typ...  12.1 us
    another operation x3, other arithmetic, local(): r_factor = jnp.linalg.cholesky(gram).T  7.98 us
  transfers between devices with their start and end apart: 8, of which 2 were waited for; matrix products, arithmetic and copies ran while one was open for 3% of the time, Pallas kernels for 0%

commit v1 on v0

v1 whole, which is shorter than its diff:
```python
import functools

import jax
import jax.numpy as jnp
from jax import lax
from jax.experimental import pallas as pl
from jax.experimental.pallas import tpu as pltpu
from jax.sharding import PartitionSpec as P

MESH = pl.DeviceIdType.MESH
HIGH = lax.Precision.HIGHEST
S = 4
Y = 8
SQ = 96


def nt(a, b, precision=None):
    return lax.dot_general(
        a, b, (((1,), (1,)), ((), ())), precision=precision, preferred_element_type=jnp.float32
    )


def nn(a, b, precision=None):
    return lax.dot_general(
        a, b, (((1,), (0,)), ((), ())), precision=precision, preferred_element_type=jnp.float32
    )


def kernel(
    dims,
    offs, delem, felem, dweight, count, rhs_hbm, blk_hbm,
    pow_hbm, r_out,
    V, B, halo, dsend, drecv, idx, coef, pbuf, s1, sy, sz, fin, linv,
    blk_sem, rhs_sem, out_sem, idx_ss, idx_rs, halo_ss, halo_rs, don_ss, don_rs, ar_ss, ar_rs,
):
    G, D, NY, NZ, E, R, W, C, total = dims
    dom, me = lax.axis_index("dom"), lax.axis_index("grid")
    core = dom % 2
    y = (dom // 2) % NY
    z = dom // (2 * NY)
    left, right = (dom + D - 1) % D, (dom + 1) % D
    grids = [(me + j) % G for j in range(G)]
    group = [
        (dom + dc * (1 - 2 * core), grids[j], (core + dc) % 2)
        for j in range(G) for dc in range(2) if (j, dc) != (0, 0)
    ]
    y_order = sorted(range(1, NY), key=lambda d: -min(d, NY - d))
    z_order = sorted(range(1, NZ), key=lambda d: -min(d, NZ - d))
    y_peers = [(z * NY + (y + d) % NY) * 2 + core for d in y_order]
    z_peers = [(((z + d) % NZ) * NY + y) * 2 + core for d in z_order]

    rhs_copy = pltpu.make_async_copy(rhs_hbm, V.at[:, pl.ds(0, R), :], rhs_sem)
    rhs_copy.start()
    blk_copies = [pltpu.make_async_copy(blk_hbm.at[e], B.at[e], blk_sem.at[e]) for e in range(E)]
    for e in [1, 2, 3, 4, 0, 5]:
        blk_copies[e].start()

    barrier = pltpu.get_barrier_semaphore()
    greeted = [(left, me), (right, me)] + [(d, g) for d, g, _ in group]
    greeted += [(d, me) for d in y_peers] + [(d, me) for d in z_peers]
    for d, g in greeted:
        pl.semaphore_signal(barrier, inc=1, device_id=(d, g), device_id_type=MESH)
    pl.semaphore_wait(barrier, len(greeted))

    pending = []

    def send(src, dst, ss, rs, dev, track=True):
        copy = pltpu.make_async_remote_copy(
            src_ref=src, dst_ref=dst, send_sem=ss, recv_sem=rs, device_id=dev, device_id_type=MESH
        )
        copy.start()
        if track:
            pending.append(copy)

    def wait_bytes(ref, sem):
        pltpu.make_async_copy(ref, ref, sem).wait()

    for j in range(1, G):
        send(delem, idx.at[G - 1 - j], idx_ss.at[j - 1], idx_rs.at[G - 1 - j], (dom, grids[j]))

    def rows(k):
        return pl.ds(k * R, R)

    def send_halo(k):
        send(V.at[0, rows(k), :], halo.at[k, 1], halo_ss.at[k, 0], halo_rs.at[k, 1], (left, me))
        send(V.at[E - 1, rows(k), :], halo.at[k, 0], halo_ss.at[k, 1], halo_rs.at[k, 0], (right, me))

    def send_donors(k):
        for j in range(1, G):
            for c in range(C):
                dsend[k, j - 1, c] = V[idx[j - 1, c, me], rows(k), :]
            send(
                dsend.at[k, j - 1], drecv.at[k, G - 1 - j],
                don_ss.at[k, j - 1], don_rs.at[k, G - 1 - j], (dom, grids[j]),
            )

    rhs_copy.wait()
    send_halo(0)

    for j in range(1, G):
        for c in range(C):
            w = jnp.where(c < count[0, grids[j]], dweight[c, grids[j]], 0.0)
            for e in range(E):
                coef[e, (j - 1) * C + c] = jnp.where(felem[c, grids[j]] == e, w, 0.0)

    linv[...] = jnp.zeros_like(linv)
    r_out[...] = jnp.zeros_like(r_out)
    pbuf[...] = jnp.zeros_like(pbuf)

    def taken(e, b, k):
        off = offs[b, e]
        if e == 0:
            own = V[jnp.maximum(off, 0), rows(k), :]
            edge = halo[k, 0]
            edge = jnp.where(dom == 0, jnp.zeros_like(edge), edge)
            return jnp.where(off < 0, edge, own)
        if e == E - 1:
            own = V[e + jnp.minimum(off, 0), rows(k), :]
            edge = halo[k, 1]
            edge = jnp.where(dom == D - 1, jnp.zeros_like(edge), edge)
            return jnp.where(off > 0, edge, own)
        return V[e + off, rows(k), :]

    NBLK = offs.shape[0]

    def product(e, k):
        lhs = jnp.concatenate([taken(e, b, k) for b in range(NBLK)], axis=-1)
        return nn(lhs, B[e])

    def panel(k):
        cols = (k + 1) * R
        acc = sum(nt(V[e, rows(k), :], V[e, pl.ds(0, cols), :]) for e in range(E))
        for h in range(2):
            pbuf[k - 1, h, :, pl.ds(0, cols)] = acc[h * 8:h * 8 + 8, :]
        if k == 1:
            acc = sum(nt(V[e, rows(0), :], V[e, rows(0), :]) for e in range(E))
            for h in range(2):
                pbuf[0, h, :, pl.ds(SQ, R)] = acc[h * 8:h * 8 + 8, :]

    def stage_1(p):
        s1[p, me * 2 + core] = pbuf[p, core]
        for d, g, c in group:
            send(
                pbuf.at[p, c], s1.at[p, me * 2 + core], ar_ss.at[p, 0], ar_rs.at[p, 0], (d, g), False
            )

    def total_of(ref, n):
        parts = [ref[i] for i in range(n)]
        while len(parts) > 1:
            parts = [a + b for a, b in zip(parts[::2], parts[1::2])] + parts[len(parts) & ~1:]
        return parts[0]

    def stage_y(p):
        wait_bytes(s1.at[p, pl.ds(0, 2 * G - 1)], ar_rs.at[p, 0])
        sy[p, y] = total_of(s1.at[p], 2 * G)
        for d in y_peers:
            send(sy.at[p, y], sy.at[p, y], ar_ss.at[p, 1], ar_rs.at[p, 1], (d, me), False)

    def stage_z(p):
        if NY > 1:
            wait_bytes(sy.at[p, pl.ds(0, NY - 1)], ar_rs.at[p, 1])
        sz[p, z] = total_of(sy.at[p], NY)
        for d in z_peers:
            send(sz.at[p, z], sz.at[p, z], ar_ss.at[p, 2], ar_rs.at[p, 2], (d, me), False)

    def stage_core(p):
        if NZ > 1:
            wait_bytes(sz.at[p, pl.ds(0, NZ - 1)], ar_rs.at[p, 2])
        fin[p, core] = total_of(sz.at[p], NZ)
        send(
            fin.at[p, core], fin.at[p, core], ar_ss.at[p, 3], ar_rs.at[p, 3],
            (dom + 1 - 2 * core, me), False,
        )

    def whole(p):
        wait_bytes(fin.at[p, 0], ar_rs.at[p, 3])
        return fin[p].reshape(R, 128) * (1.0 / total)

    lane = lax.broadcasted_iota(jnp.int32, (R, 128), 1)
    sub = lax.broadcasted_iota(jnp.int32, (R, 128), 0)

    def factor(k, pan):
        n = k * R
        rest = 128 - SQ - R
        if k == 0:
            square = jnp.where((lane >= SQ) & (lane < SQ + R), pan, 0.0)
            tab = square + jnp.where(lane == sub, 1.0, 0.0)
        else:
            left_part = jnp.where(lane < n, pan, 0.0)
            low = nt(left_part, linv[...], HIGH)
            placed = jnp.concatenate(
                [jnp.zeros((SQ, 128), jnp.float32), low, jnp.zeros((rest, 128), jnp.float32)], axis=0
            )
            square = pltpu.roll(jnp.where((lane >= n) & (lane < n + R), pan, 0.0), SQ - n, 1)
            tab = square - nt(low, placed, HIGH)
            tab = tab + jnp.where(lane == sub + n, 1.0, 0.0)
            if k < S:
                tab = tab - nn(low, linv[...], HIGH)
            turned = jnp.transpose(low)
            r_out[pl.ds(0, n), pl.ds(n, R)] = turned[:n, :]
        for j in range(R - 1):
            col = jnp.broadcast_to(tab[:, SQ + j:SQ + j + 1], (R, 128))
            mul = jnp.where(sub > j, col / col[j:j + 1, :], 0.0)
            tab = tab - mul * tab[j:j + 1, :]
        diag = jnp.sum(jnp.where(lane == sub + SQ, tab, 0.0), axis=1, keepdims=True)
        tab = tab * (1.0 / jnp.sqrt(diag))
        own = jnp.where((lane >= sub + SQ) & (lane < SQ + R), tab, 0.0)
        r_out[pl.ds(n, R), pl.ds(n, R)] = own[:, SQ:SQ + R]
        if k < S:
            linv[pl.ds(n, R), :] = jnp.where(lane < n + R, tab, 0.0)

    out_copies = []
    advance = {
        1: [],
        2: [(stage_y, 0)],
        3: [(stage_y, 1), (stage_z, 0)],
        4: [(stage_y, 2), (stage_z, 1), (stage_core, 0)],
    }
    for k in range(1, S + 1):
        prev = k - 1
        if k == 1:
            for c in [1, 2, 3, 4]:
                blk_copies[c].wait()
            for j in range(1, G):
                pltpu.make_async_remote_copy(
                    src_ref=delem, dst_ref=idx.at[j - 1], send_sem=idx_ss.at[j - 1],
                    recv_sem=idx_rs.at[j - 1], device_id=(dom, grids[j]), device_id_type=MESH,
                ).wait_recv()
            send_donors(0)
        acc = [None] * E
        for e in range(1, E - 1):
            acc[e] = product(e, prev)
        if k == 1:
            blk_copies[0].wait()
            blk_copies[E - 1].wait()
        for side in range(2):
            wait_bytes(halo.at[prev, side], halo_rs.at[prev, side])
        for e in (0, E - 1):
            acc[e] = product(e, prev)
        for j in range(1, G):
            wait_bytes(drecv.at[prev, j - 1], don_rs.at[prev, j - 1])
        for j in range(1, G):
            for c in range(C):
                donor = drecv[prev, j - 1, c].astype(jnp.float32)
                for e in range(E):
                    acc[e] = acc[e] + coef[e, (j - 1) * C + c] * donor
        for e in range(E):
            V[e, rows(k), :] = acc[e].astype(jnp.bfloat16)
        if k < S:
            send_halo(k)
            send_donors(k)
        copy = pltpu.make_async_copy(
            V.at[:, rows(k), :], pow_hbm.at[:, rows(prev), :], out_sem.at[prev]
        )
        copy.start()
        out_copies.append(copy)
        panel(k)
        stage_1(prev)
        for step, p in advance[k]:
            step(p)

    stage_y(3)
    stage_z(2)
    stage_core(1)
    first = whole(0)
    factor(0, first)
    factor(1, first)
    stage_z(3)
    stage_core(2)
    factor(2, whole(1))
    factor(3, whole(2))
    stage_core(3)
    factor(4, whole(3))

    for copy in out_copies:
        copy.wait()
    for copy in pending:
        copy.wait_send()
    for p in range(S):
        wait_bytes(s1.at[p, pl.ds(0, 2 * G - 1)], ar_ss.at[p, 0])
        if NY > 1:
            wait_bytes(sy.at[p, pl.ds(0, NY - 1)], ar_ss.at[p, 1])
        if NZ > 1:
            wait_bytes(sz.at[p, pl.ds(0, NZ - 1)], ar_ss.at[p, 2])
        wait_bytes(fin.at[p, 0], ar_ss.at[p, 3])


def solution(mesh):
    G, D = mesh.shape["grid"], mesh.shape["dom"]
    NY = Y
    NZ = D // (2 * NY)

    def local(rhs, blocks, offsets, donor_elem, fringe_elem, donor_weight, fringe_count):
        _, E, R, W = rhs.shape
        NB = blocks.shape[2]
        C = donor_elem.shape[3]
        dims = (G, D, NY, NZ, E, R, W, C, G * D * E * W)
        smem = pl.BlockSpec(memory_space=pltpu.SMEM)
        hbm = pl.BlockSpec(memory_space=pl.ANY)
        bf, f32, i32 = jnp.bfloat16, jnp.float32, jnp.int32
        dma = pltpu.SemaphoreType.DMA
        powers, r_factor = pl.pallas_call(
            functools.partial(kernel, dims),
            out_shape=(
                jax.ShapeDtypeStruct((E, S * R, W), bf),
                jax.ShapeDtypeStruct(((S + 1) * R, (S + 1) * R), f32),
            ),
            in_specs=[smem] * 5 + [hbm] * 2,
            out_specs=(hbm, pl.BlockSpec(memory_space=pltpu.VMEM)),
            scratch_shapes=[
                pltpu.VMEM((E, (S + 1) * R, W), bf),
                pltpu.VMEM((E, NB * W, W), bf),
                pltpu.VMEM((S, 2, R, W), bf),
                pltpu.VMEM((S, G - 1, C, R, W), bf),
                pltpu.VMEM((S, G - 1, C, R, W), bf),
                pltpu.SMEM((G - 1, C, G), i32),
                pltpu.SMEM((E, (G - 1) * C), f32),
                pltpu.VMEM((S, 2, 8, 128), f32),
                pltpu.VMEM((S, 2 * G, 8, 128), f32),
                pltpu.VMEM((S, NY, 8, 128), f32),
                pltpu.VMEM((S, NZ, 8, 128), f32),
                pltpu.VMEM((S, 2, 8, 128), f32),
                pltpu.VMEM((128, 128), f32),
                dma((E,)), dma(()), dma((S,)),
                dma((G - 1,)), dma((G - 1,)),
                dma((S, 2)), dma((S, 2)),
                dma((S, G - 1)), dma((S, G - 1)),
                dma((S, 4)), dma((S, 4)),
            ],
            compiler_params=pltpu.CompilerParams(
                collective_id=0, has_side_effects=True, vmem_limit_bytes=32 << 20
            ),
            name="powers_qr",
        )(
            offsets[0].T,
            donor_elem[0, 0].T,
            fringe_elem[0, 0].T,
            donor_weight[0, 0].T,
            fringe_count[0],
            rhs[0],
            blocks.reshape(E, NB * W, W),
        )
        return powers.reshape(1, E, S, R, W), r_factor

    in_specs = (
        P("grid", "dom", None, None),
        P("grid", "dom", None, None, None),
        P("grid", "dom", None),
        P("grid", "dom", None, None),
        P("grid", "dom", None, None),
        P("grid", "dom", None, None),
        P("grid", "dom", None),
    )
    out_specs = (P("grid", "dom", None, None, None), P())
    return jax.shard_map(local, mesh=mesh, in_specs=in_specs, out_specs=out_specs, check_vma=False)
```

time: 243 us -> 74.4 us (0.31)
  blocking collectives: 169 us -> 0 us
  Pallas kernels: 0 us -> 65.6 us
  starting transfers between devices: 33.7 us -> 0 us
  matrix products: 14.9 us -> 0 us
  other arithmetic: 11.8 us -> 0 us
  waiting for transfers between devices: 2.86 us -> 0 us
    psum x1 -> x0, blocking collectives: 129 us -> none  [local(): gram = lax.psum(partial_gram.reshape(columns, columns), ('dom', 'grid'))]
    pallas_call x0 -> x1, Pallas kernels: none -> 65.6 us  [local(): pl.pallas_call(functools.partial(kernel, dims), out_shape=(jax.ShapeDtype...]
    all_gather x4 -> x0, blocking collectives: 40 us -> none  [local(): gathered = lax.all_gather(field, 'grid', axis=0, tiled=True)]
    ppermute x8 -> x0, starting transfers between devices: 33.7 us -> none  [the longest x4 20.1 us: extended_2(): after = lax.ppermute(leading, axis, down)]
    dot_general x9 -> x0, matrix products: 14.9 us -> none  [the longest x4 12.1 us: local(): jnp.einsum('ekra,ekab->erb', taken_cols, blocks[0], preferred_element_typ...]
    another operation x3 -> x0, other arithmetic: 7.98 us -> none  [local(): r_factor = jnp.linalg.cholesky(gram).T]
    unnamed x5 -> x15, local copies, waits for them, and re-layouts: 2.35 us -> 7.84 us
    gather x8 -> x0, local copies, waits for them, and re-layouts: 4.68 us -> none  [the longest x4 2.4 us: local(): taken_cols = extended[col_index]]
  transfers between devices with their start and end apart: 8 -> 0, of which waited for: 2 -> 0; matrix products, arithmetic and copies ran while one was open for 3% -> 0% of each run, Pallas kernels for 0% -> 0%
where the time goes in v1:
time: 74.4 us; the launch traced here: 74.1 us
  Pallas kernels  65.6 us (88%)
  local copies, waits for them, and re-layouts  7.84 us (11%)
    pallas_call x1, Pallas kernels, local(): pl.pallas_call(functools.partial(kernel, dims), out_shape=(jax.ShapeDtype...  65.6 us
    unnamed x15, local copies, waits for them, and re-layouts  7.84 us

profile of v1, /device:TPU:1, one launch (start us, length us, event | category | flops | bytes accessed | tf_op | source)
XLA Modules:
  0.0 74.1 jit_solution(6514868420445742264)
XLA Ops:
  0.6 0.7 copy.11
  1.3 0.0 copy-start
  1.3 2.3 %copy-done = bf16[1,6,3,320,320]{4,3,2,1,0:T(8,128)(2,1)S(1)} copy-done((bf16[1,6,3,320,320]{4,3,2,1,0:T(8,128)(2,1)S(1)}, bf16[1,6,3,320,320]{4,3,2,1,0:T(8,128)(2,1)}, u32[]{:S(2)}) %copy-start) | copy-done | bytes 3686424
  3.6 0.0 copy-start.1
  3.6 0.9 %copy-done.1 = bf16[1,6,16,320]{3,2,1,0:T(8,128)(2,1)S(1)} copy-done((bf16[1,6,16,320]{3,2,1,0:T(8,128)(2,1)S(1)}, bf16[1,6,16,320]{3,2,1,0:T(8,128)(2,1)}, u32[]{:S(2)}) %copy-start.1) | copy-done | bytes 61464
  4.5 0.0 copy-start.2
  4.5 0.7 copy-done.2
  5.1 0.0 copy-start.3
  5.1 0.7 copy-done.3
  5.8 0.0 copy-start.4
  5.8 0.7 copy-done.4
  6.5 0.0 copy-start.5
  6.5 0.7 copy-done.5
  7.1 65.6 %powers_qr.1 = (bf16[6,64,320]{2,1,0:T(8,128)(2,1)S(1)}, f32[80,80]{1,0:T(8,128)S(1)}) custom-call(s32[3,6]{1,0:T(4,128)S(1)} %bitcast.21, s32[2,4]{1,0:T(2,128)S(1)} %bitcast.22, s32[2,4]{1,0:T(2,128)S(1)} %bitcast.23, f32[2,4]{1,0:T(2,128)S(1)} %bitcast.24, s32[1,4]{1,0:T(1,128)S(1)} %bitcast.25, bf16[6,16,320]{2,1,0:T(8,128)(2,1)S(1)} %bitcast.20, ...), custom_call_target="tpu_custom_call" | custom-call | tf_op jit(solution)/shard_map/powers_qr/pallas_call | solution.py:302
  72.7 0.7 copy.14
  73.5 0.6 copy.15
Async XLA Ops:
  1.3 2.3 %copy-start = (bf16[1,6,3,320,320]{4,3,2,1,0:T(8,128)(2,1)S(1)}, bf16[1,6,3,320,320]{4,3,2,1,0:T(8,128)(2,1)}, u32[]{:S(2)}) copy-start(bf16[1,6,3,320,320]{4,3,2,1,0:T(8,128)(2,1)} %param.8) | copy-start | bytes 11059204
  3.6 0.9 %copy-start.1 = (bf16[1,6,16,320]{3,2,1,0:T(8,128)(2,1)S(1)}, bf16[1,6,16,320]{3,2,1,0:T(8,128)(2,1)}, u32[]{:S(2)}) copy-start(bf16[1,6,16,320]{3,2,1,0:T(8,128)(2,1)} %param.7) | copy-start | bytes 184324
  4.5 0.7 copy-start.2
  5.1 0.7 copy-start.3
  5.8 0.7 copy-start.4
  6.5 0.7 copy-start.5

commit v2 on v1

--- a/solution.py
+++ b/solution.py
@@ -28,10 +28,12 @@
 
 def kernel(
     dims,
-    offs, delem, felem, dweight, count, rhs_hbm, blk_hbm,
+    offs_hbm, delem_hbm, felem_hbm, dweight_hbm, count_hbm, rhs_hbm, blk_hbm,
     pow_hbm, r_out,
-    V, B, halo, dsend, drecv, idx, coef, pbuf, s1, sy, sz, fin, linv,
-    blk_sem, rhs_sem, out_sem, idx_ss, idx_rs, halo_ss, halo_rs, don_ss, don_rs, ar_ss, ar_rs,
+    offs, delem, felem, dweight, count,
+    V, B, halo, dsend, drecv, idx, coef, acc, pbuf, s1, sy, sz, fin, linv,
+    tab_sem, blk_sem, rhs_sem, out_sem, idx_ss, idx_rs, halo_ss, halo_rs, don_ss, don_rs, ar_ss, ar_rs,
+    far,
 ):
     G, D, NY, NZ, E, R, W, C, total = dims
     dom, me = lax.axis_index("dom"), lax.axis_index("grid")
@@ -49,6 +51,15 @@
     y_peers = [(z * NY + (y + d) % NY) * 2 + core for d in y_order]
     z_peers = [(((z + d) % NZ) * NY + y) * 2 + core for d in z_order]
 
+    tables = [
+        pltpu.make_async_copy(src, dst, tab_sem.at[i])
+        for i, (src, dst) in enumerate([
+            (delem_hbm, delem), (offs_hbm, offs), (felem_hbm, felem), (dweight_hbm, dweight),
+            (count_hbm, count),
+        ])
+    ]
+    for copy in tables:
+        copy.start()
     rhs_copy = pltpu.make_async_copy(rhs_hbm, V.at[:, pl.ds(0, R), :], rhs_sem)
     rhs_copy.start()
     blk_copies = [pltpu.make_async_copy(blk_hbm.at[e], B.at[e], blk_sem.at[e]) for e in range(E)]
@@ -57,10 +68,35 @@
 
     barrier = pltpu.get_barrier_semaphore()
     greeted = [(left, me), (right, me)] + [(d, g) for d, g, _ in group]
-    greeted += [(d, me) for d in y_peers] + [(d, me) for d in z_peers]
-    for d, g in greeted:
-        pl.semaphore_signal(barrier, inc=1, device_id=(d, g), device_id_type=MESH)
+    rings = [(NY, lambda d: (z * NY + (y + d) % NY) * 2 + core)]
+    rings += [(NZ, lambda d: (((z + d) % NZ) * NY + y) * 2 + core)]
+    greeted += [(at(d), me) for n, at in rings if n > 1 for d in {1, n - 1}]
+
+    def greet(sem, targets):
+        for d, g in targets:
+            pl.semaphore_signal(sem, inc=1, device_id=(d, g), device_id_type=MESH)
+
+    greet(barrier, greeted)
     pl.semaphore_wait(barrier, len(greeted))
+
+    words = []
+    for i, (n, at) in enumerate(rings):
+        steps = [d for d, least in [(1, 3), (2, 5), (2, 9)] if n > least]
+        assert n <= 13
+        for r, d in enumerate(steps):
+            words.append((r, far.at[i, r], [(at(d), me), (at(n - d), me)]))
+
+    def tell(r):
+        for when, sem, targets in words:
+            if when == r:
+                greet(sem, targets)
+
+    def hear(r):
+        for when, sem, targets in words:
+            if when == r:
+                pl.semaphore_wait(sem, len(targets))
+
+    tell(0)
 
     pending = []
 
@@ -75,7 +111,9 @@
     def wait_bytes(ref, sem):
         pltpu.make_async_copy(ref, ref, sem).wait()
 
-    for j in range(1, G):
+    farthest_first = sorted(range(1, G), key=lambda j: -min(j, G - j))
+    tables[0].wait()
+    for j in farthest_first:
         send(delem, idx.at[G - 1 - j], idx_ss.at[j - 1], idx_rs.at[G - 1 - j], (dom, grids[j]))
 
     def rows(k):
@@ -86,7 +124,7 @@
         send(V.at[E - 1, rows(k), :], halo.at[k, 0], halo_ss.at[k, 1], halo_rs.at[k, 0], (right, me))
 
     def send_donors(k):
-        for j in range(1, G):
+        for j in farthest_first:
             for c in range(C):
                 dsend[k, j - 1, c] = V[idx[j - 1, c, me], rows(k), :]
             send(
@@ -97,6 +135,8 @@
     rhs_copy.wait()
     send_halo(0)
 
+    for copy in tables[1:]:
+        copy.wait()
     for j in range(1, G):
         for c in range(C):
             w = jnp.where(c < count[0, grids[j]], dweight[c, grids[j]], 0.0)
@@ -108,7 +148,7 @@
     pbuf[...] = jnp.zeros_like(pbuf)
 
     def taken(e, b, k):
-        off = offs[b, e]
+        off = offs[b, 0, e]
         if e == 0:
             own = V[jnp.maximum(off, 0), rows(k), :]
             edge = halo[k, 0]
@@ -129,13 +169,13 @@
 
     def panel(k):
         cols = (k + 1) * R
-        acc = sum(nt(V[e, rows(k), :], V[e, pl.ds(0, cols), :]) for e in range(E))
+        own = sum(nt(V[e, rows(k), :], V[e, pl.ds(0, cols), :]) for e in range(E))
         for h in range(2):
-            pbuf[k - 1, h, :, pl.ds(0, cols)] = acc[h * 8:h * 8 + 8, :]
+            pbuf[k - 1, h, :, pl.ds(0, cols)] = own[h * 8:h * 8 + 8, :]
         if k == 1:
-            acc = sum(nt(V[e, rows(0), :], V[e, rows(0), :]) for e in range(E))
+            own = sum(nt(V[e, rows(0), :], V[e, rows(0), :]) for e in range(E))
             for h in range(2):
-                pbuf[0, h, :, pl.ds(SQ, R)] = acc[h * 8:h * 8 + 8, :]
+                pbuf[0, h, :, pl.ds(SQ, R)] = own[h * 8:h * 8 + 8, :]
 
     def stage_1(p):
         s1[p, me * 2 + core] = pbuf[p, core]
@@ -227,7 +267,6 @@
                     recv_sem=idx_rs.at[j - 1], device_id=(dom, grids[j]), device_id_type=MESH,
                 ).wait_recv()
             send_donors(0)
-        acc = [None] * E
         for e in range(1, E - 1):
             acc[e] = product(e, prev)
         if k == 1:
@@ -239,16 +278,16 @@
             acc[e] = product(e, prev)
         for j in range(1, G):
             wait_bytes(drecv.at[prev, j - 1], don_rs.at[prev, j - 1])
-        for j in range(1, G):
-            for c in range(C):
-                donor = drecv[prev, j - 1, c].astype(jnp.float32)
-                for e in range(E):
-                    acc[e] = acc[e] + coef[e, (j - 1) * C + c] * donor
+        slots = [(j - 1, c) for j in range(1, G) for c in range(C)]
+        donor = [drecv[prev, j, c].astype(jnp.float32) for j, c in slots]
         for e in range(E):
-            V[e, rows(k), :] = acc[e].astype(jnp.bfloat16)
+            value = acc[e]
+            for i in range(len(slots)):
+                value = value + coef[e, i] * donor[i]
+            V[e, rows(k), :] = value.astype(jnp.bfloat16)
         if k < S:
+            send_donors(k)
             send_halo(k)
-            send_donors(k)
         copy = pltpu.make_async_copy(
             V.at[:, rows(k), :], pow_hbm.at[:, rows(prev), :], out_sem.at[prev]
         )
@@ -256,6 +295,9 @@
         out_copies.append(copy)
         panel(k)
         stage_1(prev)
+        if k < S:
+            hear(k - 1)
+            tell(k)
         for step, p in advance[k]:
             step(p)
 
@@ -270,8 +312,6 @@
     factor(2, whole(1))
     factor(3, whole(2))
     stage_core(3)
-    factor(4, whole(3))
-
     for copy in out_copies:
         copy.wait()
     for copy in pending:
@@ -283,6 +323,7 @@
         if NZ > 1:
             wait_bytes(sz.at[p, pl.ds(0, NZ - 1)], ar_ss.at[p, 2])
         wait_bytes(fin.at[p, 0], ar_ss.at[p, 3])
+    factor(4, whole(3))
 
 
 def solution(mesh):
@@ -295,8 +336,7 @@
         NB = blocks.shape[2]
         C = donor_elem.shape[3]
         dims = (G, D, NY, NZ, E, R, W, C, G * D * E * W)
-        smem = pl.BlockSpec(memory_space=pltpu.SMEM)
-        hbm = pl.BlockSpec(memory_space=pl.ANY)
+        hbm = pl.BlockSpec(memory_space=pltpu.HBM)
         bf, f32, i32 = jnp.bfloat16, jnp.float32, jnp.int32
         dma = pltpu.SemaphoreType.DMA
         powers, r_factor = pl.pallas_call(
@@ -305,9 +345,14 @@
                 jax.ShapeDtypeStruct((E, S * R, W), bf),
                 jax.ShapeDtypeStruct(((S + 1) * R, (S + 1) * R), f32),
             ),
-            in_specs=[smem] * 5 + [hbm] * 2,
-            out_specs=(hbm, pl.BlockSpec(memory_space=pltpu.VMEM)),
+            in_specs=[hbm] * 7,
+            out_specs=(pl.BlockSpec(memory_space=pl.ANY), pl.BlockSpec(memory_space=pltpu.VMEM)),
             scratch_shapes=[
+                pltpu.SMEM((NB, 1, E), i32),
+                pltpu.SMEM((C, G), i32),
+                pltpu.SMEM((C, G), i32),
+                pltpu.SMEM((C, G), f32),
+                pltpu.SMEM((1, G), i32),
                 pltpu.VMEM((E, (S + 1) * R, W), bf),
                 pltpu.VMEM((E, NB * W, W), bf),
                 pltpu.VMEM((S, 2, R, W), bf),
@@ -315,24 +360,26 @@
                 pltpu.VMEM((S, G - 1, C, R, W), bf),
                 pltpu.SMEM((G - 1, C, G), i32),
                 pltpu.SMEM((E, (G - 1) * C), f32),
+                pltpu.VMEM((E, R, W), f32),
                 pltpu.VMEM((S, 2, 8, 128), f32),
                 pltpu.VMEM((S, 2 * G, 8, 128), f32),
                 pltpu.VMEM((S, NY, 8, 128), f32),
                 pltpu.VMEM((S, NZ, 8, 128), f32),
                 pltpu.VMEM((S, 2, 8, 128), f32),
                 pltpu.VMEM((128, 128), f32),
-                dma((E,)), dma(()), dma((S,)),
+                dma((5,)), dma((E,)), dma(()), dma((S,)),
                 dma((G - 1,)), dma((G - 1,)),
                 dma((S, 2)), dma((S, 2)),
                 dma((S, G - 1)), dma((S, G - 1)),
                 dma((S, 4)), dma((S, 4)),
+                pltpu.SemaphoreType.REGULAR((2, 3)),
             ],
             compiler_params=pltpu.CompilerParams(
-                collective_id=0, has_side_effects=True, vmem_limit_bytes=32 << 20
+                collective_id=0, has_side_effects=True, vmem_limit_bytes=67_043_328
             ),
             name="powers_qr",
         )(
-            offsets[0].T,
+            offsets.transpose(2, 0, 1),
             donor_elem[0, 0].T,
             fringe_elem[0, 0].T,
             donor_weight[0, 0].T,

time: 74.4 us -> 63.7 us (0.86)
  Pallas kernels: 65.6 us -> 59.7 us
  local copies, waits for them, and re-layouts: 7.84 us -> 3.1 us
    pallas_call x1, Pallas kernels: 65.6 us -> 59.7 us  [local(): pl.pallas_call(functools.partial(kernel, dims), out_shape=(jax.ShapeDtype...]
    unnamed x15 -> x2, local copies, waits for them, and re-layouts: 7.84 us -> 3.1 us
where the time goes in v2:
time: 63.7 us; the launch traced here: 63.4 us
  Pallas kernels  59.7 us (94%)
  local copies, waits for them, and re-layouts  3.1 us (5%)
  between operations  0.64 us (1%)
    pallas_call x1, Pallas kernels, local(): pl.pallas_call(functools.partial(kernel, dims), out_shape=(jax.ShapeDtype...  59.7 us
    unnamed x2, local copies, waits for them, and re-layouts  3.1 us

profile of v2, /device:TPU:1, one launch (start us, length us, event | category | flops | bytes accessed | tf_op | source)
XLA Modules:
  0.0 63.4 jit_solution(1257371343998137341)
XLA Ops:
  0.6 59.7 %powers_qr.1 = (bf16[6,64,320]{2,1,0:T(8,128)(2,1)}, f32[80,80]{1,0:T(8,128)}) custom-call(s32[3,1,6]{2,1,0:T(1,128)} %bitcast.17, s32[2,4]{1,0:T(2,128)} %bitcast.18, s32[2,4]{1,0:T(2,128)} %bitcast.19, f32[2,4]{1,0:T(2,128)} %bitcast.20, s32[1,4]{1,0:T(1,128)} %bitcast.21, bf16[6,16,320]{2,1,0:T(8,128)(2,1)} %bitcast.16, bf16[6,960,320]{2,1,0:T(8,128)(2,1)} %bitcast.14), custom_call_target="tpu_custom_call" | custom-call | tf_op jit(solution)/shard_map/powers_qr/pallas_call | solution.py:342
  60.3 1.7 %copy.11 = bf16[1,6,4,16,320]{4,3,2,1,0:T(8,128)(2,1)} copy(bf16[1,6,4,16,320]{4,3,2,1,0:T(8,128)(2,1)} %bitcast.15) | data formatting | bytes 491520
  62.0 1.4 %copy.12 = f32[80,80]{1,0:T(8,128)} copy(f32[80,80]{1,0:T(8,128)} %get-tuple-element.9) | data formatting | bytes 51200

commit v3 on v2

--- a/solution.py
+++ b/solution.py
@@ -26,30 +26,95 @@
     )
 
 
+def column(table, j):
+    return jnp.broadcast_to(table[:, j:j + 1], table.shape)
+
+
+def eliminate(table, at):
+    n = table.shape[0]
+    lane = lax.broadcasted_iota(jnp.int32, table.shape, 1)
+    sub = lax.broadcasted_iota(jnp.int32, table.shape, 0)
+    for j in range(0, n, 2):
+        one, two = column(table, at + j), column(table, at + j + 1)
+        mul_one = jnp.where(sub > j, one * (1.0 / one[j:j + 1, :]), 0.0)
+        table = table - mul_one * table[j:j + 1, :]
+        if j + 2 < n:
+            two = two - mul_one * one[j + 1:j + 2, :]
+            mul_two = jnp.where(sub > j + 1, two * (1.0 / two[j + 1:j + 2, :]), 0.0)
+            table = table - mul_two * table[j + 1:j + 2, :]
+    pivots = jnp.sum(jnp.where(lane == sub + at, table, 0.0), axis=1, keepdims=True)
+    return table * (1.0 / jnp.sqrt(pivots))
+
+
+def factor(k, pan, linv, r_out):
+    R = pan.shape[0]
+    n = k * R
+    lane = lax.broadcasted_iota(jnp.int32, pan.shape, 1)
+    sub = lax.broadcasted_iota(jnp.int32, pan.shape, 0)
+    if k:
+        left = jnp.where(lane < n, pan, 0.0)
+        known = linv[...]
+        low = nt(left, known, HIGH)
+        r_out[pl.ds(0, n), pl.ds(n, R)] = nt(known, left, HIGH)[:n, :]
+    if k == S:
+        own = eliminate(pan[:, n:n + R] - nt(low, low, HIGH), 0)
+        triangle = lax.broadcasted_iota(jnp.int32, own.shape, 1) >= lax.broadcasted_iota(
+            jnp.int32, own.shape, 0
+        )
+        r_out[pl.ds(n, R), pl.ds(n, R)] = jnp.where(triangle, own, 0.0)
+        return
+    inside = (lane >= SQ) & (lane < SQ + R)
+    table = jnp.where(lane == sub + n, 1.0, 0.0)
+    if k == 0:
+        table = table + jnp.where(inside, pan, 0.0)
+    else:
+        placed = jnp.concatenate(
+            [jnp.zeros((SQ, S * R), jnp.float32), low, jnp.zeros((128 - SQ - R, S * R), jnp.float32)],
+            axis=0,
+        )
+        square = jnp.where(inside, pltpu.roll(pan, SQ - n, 1), 0.0)
+        table = table + square - nt(low, placed, HIGH) - nn(low, known, HIGH)
+    table = eliminate(table, SQ)
+    own = jnp.where((lane >= sub + SQ) & inside, table, 0.0)
+    r_out[pl.ds(n, R), pl.ds(n, R)] = own[:, SQ:SQ + R]
+    linv[pl.ds(n, R), :] = jnp.where(lane < n + R, table, 0.0)
+
+
+def finish(total, pow_vmem, r_part, linv, pan, pow_hbm, r_hbm, r_all, sem):
+    powers = pltpu.make_async_copy(pow_vmem, pow_hbm, sem.at[0])
+    powers.start()
+    r_all[...] = r_part[...]
+    factor(S, pan[...].reshape(-1, 128) * (1.0 / total), linv, r_all)
+    factors = pltpu.make_async_copy(r_all, r_hbm, sem.at[1])
+    factors.start()
+    factors.wait()
+    powers.wait()
+
+
 def kernel(
     dims,
     offs_hbm, delem_hbm, felem_hbm, dweight_hbm, count_hbm, rhs_hbm, blk_hbm,
-    pow_hbm, r_out,
+    pow_out, r_out, linv, last,
     offs, delem, felem, dweight, count,
-    V, B, halo, dsend, drecv, idx, coef, acc, pbuf, s1, sy, sz, fin, linv,
-    tab_sem, blk_sem, rhs_sem, out_sem, idx_ss, idx_rs, halo_ss, halo_rs, don_ss, don_rs, ar_ss, ar_rs,
+    V, B, halo, dsend, drecv, idx, coef, acc, pbuf, s1, sy, sz, fin,
+    tab_sem, blk_sem, rhs_sem, idx_ss, idx_rs, halo_ss, halo_rs, don_ss, don_rs, ar_ss, ar_rs,
     far,
 ):
     G, D, NY, NZ, E, R, W, C, total = dims
     dom, me = lax.axis_index("dom"), lax.axis_index("grid")
-    core = dom % 2
-    y = (dom // 2) % NY
-    z = dom // (2 * NY)
-    left, right = (dom + D - 1) % D, (dom + 1) % D
-    grids = [(me + j) % G for j in range(G)]
+    core = lax.rem(dom, 2)
+    y = lax.rem(lax.div(dom, 2), NY)
+    z = lax.div(dom, 2 * NY)
+    left, right = lax.rem(dom + D - 1, D), lax.rem(dom + 1, D)
+    grids = [me] + [lax.rem(me + j, G) for j in range(1, G)]
     group = [
-        (dom + dc * (1 - 2 * core), grids[j], (core + dc) % 2)
+        (dom + dc * (1 - 2 * core), grids[j], core + dc * (1 - 2 * core))
         for j in range(G) for dc in range(2) if (j, dc) != (0, 0)
     ]
     y_order = sorted(range(1, NY), key=lambda d: -min(d, NY - d))
     z_order = sorted(range(1, NZ), key=lambda d: -min(d, NZ - d))
-    y_peers = [(z * NY + (y + d) % NY) * 2 + core for d in y_order]
-    z_peers = [(((z + d) % NZ) * NY + y) * 2 + core for d in z_order]
+    y_peers = [(z * NY + lax.rem(y + d, NY)) * 2 + core for d in y_order]
+    z_peers = [(lax.rem(z + d, NZ) * NY + y) * 2 + core for d in z_order]
 
     tables = [
         pltpu.make_async_copy(src, dst, tab_sem.at[i])
@@ -68,8 +133,8 @@
 
     barrier = pltpu.get_barrier_semaphore()
     greeted = [(left, me), (right, me)] + [(d, g) for d, g, _ in group]
-    rings = [(NY, lambda d: (z * NY + (y + d) % NY) * 2 + core)]
-    rings += [(NZ, lambda d: (((z + d) % NZ) * NY + y) * 2 + core)]
+    rings = [(NY, lambda d: (z * NY + lax.rem(y + d, NY)) * 2 + core)]
+    rings += [(NZ, lambda d: (lax.rem(z + d, NZ) * NY + y) * 2 + core)]
     greeted += [(at(d), me) for n, at in rings if n > 1 for d in {1, n - 1}]
 
     def greet(sem, targets):
@@ -149,12 +214,12 @@
 
     def taken(e, b, k):
         off = offs[b, 0, e]
-        if e == 0:
+        if isinstance(e, int) and e == 0:
             own = V[jnp.maximum(off, 0), rows(k), :]
             edge = halo[k, 0]
             edge = jnp.where(dom == 0, jnp.zeros_like(edge), edge)
             return jnp.where(off < 0, edge, own)
-        if e == E - 1:
+        if isinstance(e, int) and e == E - 1:
             own = V[e + jnp.minimum(off, 0), rows(k), :]
             edge = halo[k, 1]
             edge = jnp.where(dom == D - 1, jnp.zeros_like(edge), edge)
@@ -212,49 +277,17 @@
             (dom + 1 - 2 * core, me), False,
         )
 
+    def arrived(p):
+        wait_bytes(fin.at[p, 0], ar_rs.at[p, 3])
+
     def whole(p):
-        wait_bytes(fin.at[p, 0], ar_rs.at[p, 3])
         return fin[p].reshape(R, 128) * (1.0 / total)
 
-    lane = lax.broadcasted_iota(jnp.int32, (R, 128), 1)
-    sub = lax.broadcasted_iota(jnp.int32, (R, 128), 0)
-
-    def factor(k, pan):
-        n = k * R
-        rest = 128 - SQ - R
-        if k == 0:
-            square = jnp.where((lane >= SQ) & (lane < SQ + R), pan, 0.0)
-            tab = square + jnp.where(lane == sub, 1.0, 0.0)
-        else:
-            left_part = jnp.where(lane < n, pan, 0.0)
-            low = nt(left_part, linv[...], HIGH)
-            placed = jnp.concatenate(
-                [jnp.zeros((SQ, 128), jnp.float32), low, jnp.zeros((rest, 128), jnp.float32)], axis=0
-            )
-            square = pltpu.roll(jnp.where((lane >= n) & (lane < n + R), pan, 0.0), SQ - n, 1)
-            tab = square - nt(low, placed, HIGH)
-            tab = tab + jnp.where(lane == sub + n, 1.0, 0.0)
-            if k < S:
-                tab = tab - nn(low, linv[...], HIGH)
-            turned = jnp.transpose(low)
-            r_out[pl.ds(0, n), pl.ds(n, R)] = turned[:n, :]
-        for j in range(R - 1):
-            col = jnp.broadcast_to(tab[:, SQ + j:SQ + j + 1], (R, 128))
-            mul = jnp.where(sub > j, col / col[j:j + 1, :], 0.0)
-            tab = tab - mul * tab[j:j + 1, :]
-        diag = jnp.sum(jnp.where(lane == sub + SQ, tab, 0.0), axis=1, keepdims=True)
-        tab = tab * (1.0 / jnp.sqrt(diag))
-        own = jnp.where((lane >= sub + SQ) & (lane < SQ + R), tab, 0.0)
-        r_out[pl.ds(n, R), pl.ds(n, R)] = own[:, SQ:SQ + R]
-        if k < S:
-            linv[pl.ds(n, R), :] = jnp.where(lane < n + R, tab, 0.0)
-
-    out_copies = []
     advance = {
         1: [],
         2: [(stage_y, 0)],
         3: [(stage_y, 1), (stage_z, 0)],
-        4: [(stage_y, 2), (stage_z, 1), (stage_core, 0)],
+        4: [(stage_y, 2), (stage_z, 1)],
     }
     for k in range(1, S + 1):
         prev = k - 1
@@ -267,32 +300,31 @@
                     recv_sem=idx_rs.at[j - 1], device_id=(dom, grids[j]), device_id_type=MESH,
                 ).wait_recv()
             send_donors(0)
-        for e in range(1, E - 1):
-            acc[e] = product(e, prev)
+        def inner(i, carry):
+            for e in (2 * i + 1, 2 * i + 2):
+                acc[e] = product(e, prev)
+            return carry
+
+        lax.fori_loop(0, E // 2 - 1, inner, 0)
         if k == 1:
             blk_copies[0].wait()
             blk_copies[E - 1].wait()
-        for side in range(2):
+        for side, e in ((0, 0), (1, E - 1)):
             wait_bytes(halo.at[prev, side], halo_rs.at[prev, side])
-        for e in (0, E - 1):
             acc[e] = product(e, prev)
         for j in range(1, G):
             wait_bytes(drecv.at[prev, j - 1], don_rs.at[prev, j - 1])
         slots = [(j - 1, c) for j in range(1, G) for c in range(C)]
         donor = [drecv[prev, j, c].astype(jnp.float32) for j, c in slots]
-        for e in range(E):
+        for e in (0, E - 1, *range(1, E - 1)):
             value = acc[e]
             for i in range(len(slots)):
                 value = value + coef[e, i] * donor[i]
             V[e, rows(k), :] = value.astype(jnp.bfloat16)
+            if e == E - 1 and k < S:
+                send_halo(k)
         if k < S:
             send_donors(k)
-            send_halo(k)
-        copy = pltpu.make_async_copy(
-            V.at[:, rows(k), :], pow_hbm.at[:, rows(prev), :], out_sem.at[prev]
-        )
-        copy.start()
-        out_copies.append(copy)
         panel(k)
         stage_1(prev)
         if k < S:
@@ -300,20 +332,22 @@
             tell(k)
         for step, p in advance[k]:
             step(p)
-
+        pow_out[:, rows(prev), :] = V[:, rows(k), :]
+
+    stage_core(0)
     stage_y(3)
     stage_z(2)
+    arrived(0)
+    factor(0, whole(0), linv, r_out)
     stage_core(1)
-    first = whole(0)
-    factor(0, first)
-    factor(1, first)
     stage_z(3)
+    factor(1, whole(0), linv, r_out)
+    arrived(1)
+    factor(2, whole(1), linv, r_out)
     stage_core(2)
-    factor(2, whole(1))
-    factor(3, whole(2))
+    arrived(2)
+    factor(3, whole(2), linv, r_out)
     stage_core(3)
-    for copy in out_copies:
-        copy.wait()
     for copy in pending:
         copy.wait_send()
     for p in range(S):
@@ -323,7 +357,8 @@
         if NZ > 1:
             wait_bytes(sz.at[p, pl.ds(0, NZ - 1)], ar_ss.at[p, 2])
         wait_bytes(fin.at[p, 0], ar_ss.at[p, 3])
-    factor(4, whole(3))
+    arrived(3)
+    last[...] = fin[3]
 
 
 def solution(mesh):
@@ -337,16 +372,20 @@
         C = donor_elem.shape[3]
         dims = (G, D, NY, NZ, E, R, W, C, G * D * E * W)
         hbm = pl.BlockSpec(memory_space=pltpu.HBM)
+        any_space = pl.BlockSpec(memory_space=pl.ANY)
+        vmem = pl.BlockSpec(memory_space=pltpu.VMEM)
         bf, f32, i32 = jnp.bfloat16, jnp.float32, jnp.int32
         dma = pltpu.SemaphoreType.DMA
-        powers, r_factor = pl.pallas_call(
+        state = pl.pallas_call(
             functools.partial(kernel, dims),
             out_shape=(
-                jax.ShapeDtypeStruct((E, S * R, W), bf),
-                jax.ShapeDtypeStruct(((S + 1) * R, (S + 1) * R), f32),
+                pltpu.VMEM((E, S * R, W), bf),
+                pltpu.VMEM(((S + 1) * R, (S + 1) * R), f32),
+                pltpu.VMEM((S * R, 128), f32),
+                pltpu.VMEM((2, 8, 128), f32),
             ),
             in_specs=[hbm] * 7,
-            out_specs=(pl.BlockSpec(memory_space=pl.ANY), pl.BlockSpec(memory_space=pltpu.VMEM)),
+            out_specs=(vmem,) * 4,
             scratch_shapes=[
                 pltpu.SMEM((NB, 1, E), i32),
                 pltpu.SMEM((C, G), i32),
@@ -366,8 +405,7 @@
                 pltpu.VMEM((S, NY, 8, 128), f32),
                 pltpu.VMEM((S, NZ, 8, 128), f32),
                 pltpu.VMEM((S, 2, 8, 128), f32),
-                pltpu.VMEM((128, 128), f32),
-                dma((5,)), dma((E,)), dma(()), dma((S,)),
+                dma((5,)), dma((E,)), dma(()),
                 dma((G - 1,)), dma((G - 1,)),
                 dma((S, 2)), dma((S, 2)),
                 dma((S, G - 1)), dma((S, G - 1)),
@@ -375,7 +413,7 @@
                 pltpu.SemaphoreType.REGULAR((2, 3)),
             ],
             compiler_params=pltpu.CompilerParams(
-                collective_id=0, has_side_effects=True, vmem_limit_bytes=67_043_328
+                collective_id=0, has_side_effects=True, vmem_limit_bytes=60 << 20
             ),
             name="powers_qr",
         )(
@@ -387,6 +425,18 @@
             rhs[0],
             blocks.reshape(E, NB * W, W),
         )
+        powers, r_factor = pl.pallas_call(
+            functools.partial(finish, G * D * E * W),
+            out_shape=(
+                jax.ShapeDtypeStruct((E, S * R, W), bf),
+                jax.ShapeDtypeStruct(((S + 1) * R, (S + 1) * R), f32),
+            ),
+            in_specs=[any_space, vmem, vmem, vmem],
+            out_specs=(any_space, any_space),
+            scratch_shapes=[pltpu.VMEM(((S + 1) * R, (S + 1) * R), f32), dma((2,))],
+            compiler_params=pltpu.CompilerParams(vmem_limit_bytes=2 << 20),
+            name="finish",
+        )(*state)
         return powers.reshape(1, E, S, R, W), r_factor
 
     in_specs = (

time: 63.7 us -> 56.4 us (0.89)
  Pallas kernels: 59.7 us -> 55.6 us
  local copies, waits for them, and re-layouts: 3.1 us -> 0 us
    pallas_call x1 -> x2, Pallas kernels: 59.7 us -> 55.6 us  [the longest x1 53.4 us: local(): pl.pallas_call(functools.partial(kernel, dims), out_shape=(pltpu.VMEM((E,...]
    unnamed x2 -> x0, local copies, waits for them, and re-layouts: 3.1 us -> none
where the time goes in v3:
time: 56.4 us; the launch traced here: 56.3 us
  Pallas kernels  55.6 us (99%)
  between operations  0.64 us (1%)
    pallas_call x1, Pallas kernels, local(): pl.pallas_call(functools.partial(kernel, dims), out_shape=(pltpu.VMEM((E,...  53.4 us
    pallas_call x1, Pallas kernels, local(): pl.pallas_call(functools.partial(finish, G * D * E * W), out_shape=(jax.S...  2.26 us

profile of v3, /device:TPU:1, one launch (start us, length us, event | category | flops | bytes accessed | tf_op | source)
XLA Modules:
  0.0 56.3 jit_solution(11758074411870209370)
XLA Ops:
  0.6 53.4 %powers_qr.1 = (bf16[6,64,320]{2,1,0:T(8,128)(2,1)S(1)}, f32[80,80]{1,0:T(8,128)S(1)}, f32[64,128]{1,0:T(8,128)S(1)}, f32[2,8,128]{2,1,0:T(8,128)S(1)}) custom-call(s32[3,1,6]{2,1,0:T(1,128)} %bitcast.16, s32[2,4]{1,0:T(2,128)} %bitcast.17, s32[2,4]{1,0:T(2,128)} %bitcast.18, f32[2,4]{1,0:T(2,128)} %bitcast.19, s32[1,4]{1,0:T(1,128)} %bitcast.20, ...), custom_call_target="tpu_custom_call" | custom-call | tf_op jit(solution)/shard_map/powers_qr/pallas_call | solution.py:379
  54.0 2.3 %finish.1 = (bf16[6,64,320]{2,1,0:T(8,128)(2,1)}, f32[80,80]{1,0:T(8,128)}) custom-call(bf16[6,64,320]{2,1,0:T(8,128)(2,1)S(1)} %get-tuple-element.8.pow_vmem, f32[80,80]{1,0:T(8,128)S(1)} %get-tuple-element.9.r_part, f32[64,128]{1,0:T(8,128)S(1)} %get-tuple-element.10.linv, f32[2,8,128]{2,1,0:T(8,128)S(1)} %get-tuple-element.11.pan), custom_call_target="tpu_custom_call" | custom-call | tf_op jit(solution)/shard_map/finish/pallas_call | solution.py:428

commit v4 on v3

--- a/solution.py
+++ b/solution.py
@@ -24,6 +24,15 @@
     return lax.dot_general(
         a, b, (((1,), (0,)), ((), ())), precision=precision, preferred_element_type=jnp.float32
     )
+
+
+def wrap(i, n):
+    for shift in range(1, 20):
+        power = 1 << shift
+        scale = -(-power // n)
+        if all(v * scale // power == v // n for v in range(2 * n)):
+            return i - n * lax.div(i * scale, power)
+    return lax.rem(i, n)
 
 
 def column(table, j):
@@ -105,16 +114,28 @@
     core = lax.rem(dom, 2)
     y = lax.rem(lax.div(dom, 2), NY)
     z = lax.div(dom, 2 * NY)
-    left, right = lax.rem(dom + D - 1, D), lax.rem(dom + 1, D)
-    grids = [me] + [lax.rem(me + j, G) for j in range(1, G)]
+    left, right = wrap(dom + D - 1, D), wrap(dom + 1, D)
+    grids = [me] + [wrap(me + j, G) for j in range(1, G)]
     group = [
-        (dom + dc * (1 - 2 * core), grids[j], core + dc * (1 - 2 * core))
+        (dom + dc * (1 - 2 * core), grids[j])
         for j in range(G) for dc in range(2) if (j, dc) != (0, 0)
     ]
     y_order = sorted(range(1, NY), key=lambda d: -min(d, NY - d))
     z_order = sorted(range(1, NZ), key=lambda d: -min(d, NZ - d))
-    y_peers = [(z * NY + lax.rem(y + d, NY)) * 2 + core for d in y_order]
-    z_peers = [(lax.rem(z + d, NZ) * NY + y) * 2 + core for d in z_order]
+    y_peers = [(z * NY + wrap(y + d, NY)) * 2 + core for d in y_order]
+    z_peers = [(wrap(z + d, NZ) * NY + y) * 2 + core for d in z_order]
+
+    barrier = pltpu.get_barrier_semaphore()
+    greeted = [(left, me), (right, me)] + group
+    rings = [(NY, lambda d: (z * NY + wrap(y + d, NY)) * 2 + core)]
+    rings += [(NZ, lambda d: (wrap(z + d, NZ) * NY + y) * 2 + core)]
+    greeted += [(at(d), me) for n, at in rings if n > 1 for d in {1, n - 1}]
+
+    def greet(sem, targets):
+        for d, g in targets:
+            pl.semaphore_signal(sem, inc=1, device_id=(d, g), device_id_type=MESH)
+
+    greet(barrier, greeted)
 
     tables = [
         pltpu.make_async_copy(src, dst, tab_sem.at[i])
@@ -131,17 +152,6 @@
     for e in [1, 2, 3, 4, 0, 5]:
         blk_copies[e].start()
 
-    barrier = pltpu.get_barrier_semaphore()
-    greeted = [(left, me), (right, me)] + [(d, g) for d, g, _ in group]
-    rings = [(NY, lambda d: (z * NY + lax.rem(y + d, NY)) * 2 + core)]
-    rings += [(NZ, lambda d: (lax.rem(z + d, NZ) * NY + y) * 2 + core)]
-    greeted += [(at(d), me) for n, at in rings if n > 1 for d in {1, n - 1}]
-
-    def greet(sem, targets):
-        for d, g in targets:
-            pl.semaphore_signal(sem, inc=1, device_id=(d, g), device_id_type=MESH)
-
-    greet(barrier, greeted)
     pl.semaphore_wait(barrier, len(greeted))
 
     words = []
@@ -243,10 +253,10 @@
                 pbuf[0, h, :, pl.ds(SQ, R)] = own[h * 8:h * 8 + 8, :]
 
     def stage_1(p):
-        s1[p, me * 2 + core] = pbuf[p, core]
-        for d, g, c in group:
+        s1[p, me * 2 + core] = pbuf[p]
+        for d, g in group:
             send(
-                pbuf.at[p, c], s1.at[p, me * 2 + core], ar_ss.at[p, 0], ar_rs.at[p, 0], (d, g), False
+                pbuf.at[p], s1.at[p, me * 2 + core], ar_ss.at[p, 0], ar_rs.at[p, 0], (d, g), False
             )
 
     def total_of(ref, n):
@@ -268,17 +278,10 @@
         for d in z_peers:
             send(sz.at[p, z], sz.at[p, z], ar_ss.at[p, 2], ar_rs.at[p, 2], (d, me), False)
 
-    def stage_core(p):
+    def stage_end(p):
         if NZ > 1:
             wait_bytes(sz.at[p, pl.ds(0, NZ - 1)], ar_rs.at[p, 2])
-        fin[p, core] = total_of(sz.at[p], NZ)
-        send(
-            fin.at[p, core], fin.at[p, core], ar_ss.at[p, 3], ar_rs.at[p, 3],
-            (dom + 1 - 2 * core, me), False,
-        )
-
-    def arrived(p):
-        wait_bytes(fin.at[p, 0], ar_rs.at[p, 3])
+        fin[p] = total_of(sz.at[p], NZ)
 
     def whole(p):
         return fin[p].reshape(R, 128) * (1.0 / total)
@@ -334,20 +337,16 @@
             step(p)
         pow_out[:, rows(prev), :] = V[:, rows(k), :]
 
-    stage_core(0)
     stage_y(3)
+    stage_end(0)
+    factor(0, whole(0), linv, r_out)
     stage_z(2)
-    arrived(0)
-    factor(0, whole(0), linv, r_out)
-    stage_core(1)
+    factor(1, whole(0), linv, r_out)
     stage_z(3)
-    factor(1, whole(0), linv, r_out)
-    arrived(1)
+    stage_end(1)
     factor(2, whole(1), linv, r_out)
-    stage_core(2)
-    arrived(2)
+    stage_end(2)
     factor(3, whole(2), linv, r_out)
-    stage_core(3)
     for copy in pending:
         copy.wait_send()
     for p in range(S):
@@ -356,8 +355,7 @@
             wait_bytes(sy.at[p, pl.ds(0, NY - 1)], ar_ss.at[p, 1])
         if NZ > 1:
             wait_bytes(sz.at[p, pl.ds(0, NZ - 1)], ar_ss.at[p, 2])
-        wait_bytes(fin.at[p, 0], ar_ss.at[p, 3])
-    arrived(3)
+    stage_end(3)
     last[...] = fin[3]
 
 
@@ -401,15 +399,15 @@
                 pltpu.SMEM((E, (G - 1) * C), f32),
                 pltpu.VMEM((E, R, W), f32),
                 pltpu.VMEM((S, 2, 8, 128), f32),
-                pltpu.VMEM((S, 2 * G, 8, 128), f32),
-                pltpu.VMEM((S, NY, 8, 128), f32),
-                pltpu.VMEM((S, NZ, 8, 128), f32),
+                pltpu.VMEM((S, 2 * G, 2, 8, 128), f32),
+                pltpu.VMEM((S, NY, 2, 8, 128), f32),
+                pltpu.VMEM((S, NZ, 2, 8, 128), f32),
                 pltpu.VMEM((S, 2, 8, 128), f32),
                 dma((5,)), dma((E,)), dma(()),
                 dma((G - 1,)), dma((G - 1,)),
                 dma((S, 2)), dma((S, 2)),
                 dma((S, G - 1)), dma((S, G - 1)),
-                dma((S, 4)), dma((S, 4)),
+                dma((S, 3)), dma((S, 3)),
                 pltpu.SemaphoreType.REGULAR((2, 3)),
             ],
             compiler_params=pltpu.CompilerParams(

time: 56.4 us -> 54.2 us (0.961)
  Pallas kernels: 55.6 us -> 53.4 us
    pallas_call x1, Pallas kernels: 53.4 us -> 51.1 us  [local(): pl.pallas_call(functools.partial(kernel, dims), out_shape=(pltpu.VMEM((E,...]
where the time goes in v4:
time: 54.2 us; the launch traced here: 54 us
  Pallas kernels  53.4 us (99%)
  between operations  0.64 us (1%)
    pallas_call x1, Pallas kernels, local(): pl.pallas_call(functools.partial(kernel, dims), out_shape=(pltpu.VMEM((E,...  51.1 us
    pallas_call x1, Pallas kernels, local(): pl.pallas_call(functools.partial(finish, G * D * E * W), out_shape=(jax.S...  2.26 us

profile of v4, /device:TPU:1, one launch (start us, length us, event | category | flops | bytes accessed | tf_op | source)
XLA Modules:
  0.0 54.0 jit_solution(15519561480448902824)
XLA Ops:
  0.6 51.1 %powers_qr.1 = (bf16[6,64,320]{2,1,0:T(8,128)(2,1)S(1)}, f32[80,80]{1,0:T(8,128)S(1)}, f32[64,128]{1,0:T(8,128)S(1)}, f32[2,8,128]{2,1,0:T(8,128)S(1)}) custom-call(s32[3,1,6]{2,1,0:T(1,128)} %bitcast.16, s32[2,4]{1,0:T(2,128)} %bitcast.17, s32[2,4]{1,0:T(2,128)} %bitcast.18, f32[2,4]{1,0:T(2,128)} %bitcast.19, s32[1,4]{1,0:T(1,128)} %bitcast.20, ...), custom_call_target="tpu_custom_call" | custom-call | tf_op jit(solution)/shard_map/powers_qr/pallas_call | solution.py:377
  51.8 2.3 %finish.1 = (bf16[6,64,320]{2,1,0:T(8,128)(2,1)}, f32[80,80]{1,0:T(8,128)}) custom-call(bf16[6,64,320]{2,1,0:T(8,128)(2,1)S(1)} %get-tuple-element.8.pow_vmem, f32[80,80]{1,0:T(8,128)S(1)} %get-tuple-element.9.r_part, f32[64,128]{1,0:T(8,128)S(1)} %get-tuple-element.10.linv, f32[2,8,128]{2,1,0:T(8,128)S(1)} %get-tuple-element.11.pan), custom_call_target="tpu_custom_call" | custom-call | tf_op jit(solution)/shard_map/finish/pallas_call | solution.py:426

commit v5 on v4

--- a/solution.py
+++ b/solution.py
@@ -125,18 +125,6 @@
     y_peers = [(z * NY + wrap(y + d, NY)) * 2 + core for d in y_order]
     z_peers = [(wrap(z + d, NZ) * NY + y) * 2 + core for d in z_order]
 
-    barrier = pltpu.get_barrier_semaphore()
-    greeted = [(left, me), (right, me)] + group
-    rings = [(NY, lambda d: (z * NY + wrap(y + d, NY)) * 2 + core)]
-    rings += [(NZ, lambda d: (wrap(z + d, NZ) * NY + y) * 2 + core)]
-    greeted += [(at(d), me) for n, at in rings if n > 1 for d in {1, n - 1}]
-
-    def greet(sem, targets):
-        for d, g in targets:
-            pl.semaphore_signal(sem, inc=1, device_id=(d, g), device_id_type=MESH)
-
-    greet(barrier, greeted)
-
     tables = [
         pltpu.make_async_copy(src, dst, tab_sem.at[i])
         for i, (src, dst) in enumerate([
@@ -144,10 +132,24 @@
             (count_hbm, count),
         ])
     ]
-    for copy in tables:
-        copy.start()
+    tables[0].start()
     rhs_copy = pltpu.make_async_copy(rhs_hbm, V.at[:, pl.ds(0, R), :], rhs_sem)
     rhs_copy.start()
+
+    barrier = pltpu.get_barrier_semaphore()
+    greeted = [(left, me), (right, me)] + group
+    rings = [(NY, lambda d: (z * NY + wrap(y + d, NY)) * 2 + core)]
+    rings += [(NZ, lambda d: (wrap(z + d, NZ) * NY + y) * 2 + core)]
+    greeted += [(at(d), me) for n, at in rings if n > 1 for d in {1, n - 1}]
+
+    def greet(sem, targets):
+        for d, g in targets:
+            pl.semaphore_signal(sem, inc=1, device_id=(d, g), device_id_type=MESH)
+
+    greet(barrier, greeted)
+
+    for copy in tables[1:]:
+        copy.start()
     blk_copies = [pltpu.make_async_copy(blk_hbm.at[e], B.at[e], blk_sem.at[e]) for e in range(E)]
     for e in [1, 2, 3, 4, 0, 5]:
         blk_copies[e].start()
@@ -170,8 +172,6 @@
         for when, sem, targets in words:
             if when == r:
                 pl.semaphore_wait(sem, len(targets))
-
-    tell(0)
 
     pending = []
 
@@ -209,6 +209,7 @@
 
     rhs_copy.wait()
     send_halo(0)
+    tell(0)
 
     for copy in tables[1:]:
         copy.wait()

time: 54.2 us -> 54.2 us (level)
  no operation moved by 1% of the time
where the time goes in v5:
time: 54.2 us; the launch traced here: 54 us
  Pallas kernels  53.4 us (99%)
  between operations  0.64 us (1%)
    pallas_call x1, Pallas kernels, local(): pl.pallas_call(functools.partial(kernel, dims), out_shape=(pltpu.VMEM((E,...  51.1 us
    pallas_call x1, Pallas kernels, local(): pl.pallas_call(functools.partial(finish, G * D * E * W), out_shape=(jax.S...  2.26 us

profile of v5, /device:TPU:1, one launch (start us, length us, event | category | flops | bytes accessed | tf_op | source)
XLA Modules:
  0.0 54.0 jit_solution(17997345536133695332)
XLA Ops:
  0.6 51.1 %powers_qr.1 = (bf16[6,64,320]{2,1,0:T(8,128)(2,1)S(1)}, f32[80,80]{1,0:T(8,128)S(1)}, f32[64,128]{1,0:T(8,128)S(1)}, f32[2,8,128]{2,1,0:T(8,128)S(1)}) custom-call(s32[3,1,6]{2,1,0:T(1,128)} %bitcast.16, s32[2,4]{1,0:T(2,128)} %bitcast.17, s32[2,4]{1,0:T(2,128)} %bitcast.18, f32[2,4]{1,0:T(2,128)} %bitcast.19, s32[1,4]{1,0:T(1,128)} %bitcast.20, ...), custom_call_target="tpu_custom_call" | custom-call | tf_op jit(solution)/shard_map/powers_qr/pallas_call | solution.py:378
  51.8 2.3 %finish.1 = (bf16[6,64,320]{2,1,0:T(8,128)(2,1)}, f32[80,80]{1,0:T(8,128)}) custom-call(bf16[6,64,320]{2,1,0:T(8,128)(2,1)S(1)} %get-tuple-element.8.pow_vmem, f32[80,80]{1,0:T(8,128)S(1)} %get-tuple-element.9.r_part, f32[64,128]{1,0:T(8,128)S(1)} %get-tuple-element.10.linv, f32[2,8,128]{2,1,0:T(8,128)S(1)} %get-tuple-element.11.pan), custom_call_target="tpu_custom_call" | custom-call | tf_op jit(solution)/shard_map/finish/pallas_call | solution.py:427
